TPU v7x, 512 devices: a whole 4x8x8 slice. The times are simulated.
512 devices in a mesh: dp: 4 (over y_lo), seq: 32 (over z, y_hi, core), tensor: 4 (over x).
Axes of the slice: x: 4, y: 8 (y_hi: 2, y_lo: 4; y = y_hi * 4 + y_lo), z: 8, core: 2. Of those that a mesh axis runs over, the one named last changes fastest.
Arguments:
- queries: bfloat16 [4, 16384, 512], P('dp', 'seq', 'tensor'), may hold values from -6 to 6
- values: bfloat16 [4, 16384, 512], P('dp', 'seq', 'tensor'), may hold values from -6 to 6
- filt: float32 [16384, 512], P('seq', 'tensor'), may hold values from -4 to 4
- w_out: bfloat16 [512, 4096], P('tensor'), may hold values from -0.375 to 0.375
- cotangent: bfloat16 [4, 16384, 4096], P('dp', 'seq', 'tensor'), may hold values from -6 to 6
Outputs:
- mixed: bfloat16 [4, 16384, 4096], P('dp', 'seq', 'tensor')
- grad_query: bfloat16 [4, 16384, 512], P('dp', 'seq', 'tensor')
- grad_value: bfloat16 [4, 16384, 512], P('dp', 'seq', 'tensor')
- grad_filt: float32 [16384, 512], P('seq', 'tensor')
All inputs are finite; a program needn't handle non-finite values.
Results may differ from a plain program's by a relative error of at most 0.024.
Values may be sent and summed in bfloat16 or wider, within the bound.
No kernel may reach another device: no remote copies, remote signals or barrier semaphores. Data moves between devices by JAX's collectives and lax.ppermute only.
A program may use at most 64 MiB of HBM per device.

v0:
```python
import math
import jax
import jax.numpy as jnp
from jax import lax
from jax.sharding import PartitionSpec as P

HIGHEST = lax.Precision.HIGHEST


def for_sending(array):
    return jax.tree.map(lambda a: a.astype(jnp.bfloat16) if a.dtype == jnp.float32 else a, array)


def angle_table(first, second, period):
    index = first[:, None] * second[None, :] % period
    angle = -2.0 * math.pi / period * index.astype(jnp.float32)
    return (jnp.cos(angle), jnp.sin(angle))


def product(table_real, table_imag, data_real, data_imag, form):

    def apply(left, right):
        return jnp.einsum(form, left, right, precision=HIGHEST)

    return (
        apply(table_real, data_real) - apply(table_imag, data_imag),
        apply(table_real, data_imag) + apply(table_imag, data_real),
    )


def split_length(length):
    levels = length.bit_length() - 1
    inner = 1 << levels // 2
    return (inner, length // inner)


def local_forward(data_real, data_imag, freq_index, total):
    pair, length, width = data_real.shape
    inner, outer = split_length(length)
    cos_t, sin_t = angle_table(freq_index, jnp.arange(length, dtype=jnp.int32), total)
    cos_t = cos_t[:, :, None]
    sin_t = sin_t[:, :, None]
    data_real, data_imag = (
        data_real * cos_t - data_imag * sin_t,
        data_real * sin_t + data_imag * cos_t,
    )
    data_real = data_real.reshape(pair, outer, inner, width)
    data_imag = data_imag.reshape(pair, outer, inner, width)
    outer_c, outer_s = angle_table(
        jnp.arange(outer, dtype=jnp.int32), jnp.arange(outer, dtype=jnp.int32), outer
    )
    data_real, data_imag = product(outer_c, outer_s, data_real, data_imag, "ab,ebcd->eacd")
    mid_c, mid_s = angle_table(
        jnp.arange(outer, dtype=jnp.int32), jnp.arange(inner, dtype=jnp.int32), length
    )
    mid_c = mid_c[None, :, :, None]
    mid_s = mid_s[None, :, :, None]
    data_real, data_imag = (
        data_real * mid_c - data_imag * mid_s,
        data_real * mid_s + data_imag * mid_c,
    )
    inner_c, inner_s = angle_table(
        jnp.arange(inner, dtype=jnp.int32), jnp.arange(inner, dtype=jnp.int32), inner
    )
    return product(inner_c, inner_s, data_real, data_imag, "ab,ecbd->ecad")


def local_inverse(spec_real, spec_imag, freq_index, total):
    pair, outer, inner, width = spec_real.shape
    length = outer * inner
    inner_c, inner_s = angle_table(
        jnp.arange(inner, dtype=jnp.int32), jnp.arange(inner, dtype=jnp.int32), inner
    )
    data_real, data_imag = product(
        inner_c / inner, -inner_s / inner, spec_real, spec_imag, "ab,ecbd->ecad"
    )
    mid_c, mid_s = angle_table(
        jnp.arange(outer, dtype=jnp.int32), jnp.arange(inner, dtype=jnp.int32), length
    )
    mid_c = mid_c[None, :, :, None]
    mid_s = mid_s[None, :, :, None]
    data_real, data_imag = (
        data_real * mid_c + data_imag * mid_s,
        data_imag * mid_c - data_real * mid_s,
    )
    outer_c, outer_s = angle_table(
        jnp.arange(outer, dtype=jnp.int32), jnp.arange(outer, dtype=jnp.int32), outer
    )
    data_real, data_imag = product(
        outer_c / outer, -outer_s / outer, data_real, data_imag, "ab,ebcd->eacd"
    )
    data_real = data_real.reshape(pair, length, width)
    data_imag = data_imag.reshape(pair, length, width)
    cos_t, sin_t = angle_table(freq_index, jnp.arange(length, dtype=jnp.int32), total)
    cos_t = cos_t[:, :, None]
    sin_t = sin_t[:, :, None]
    return (data_real * cos_t + data_imag * sin_t, data_imag * cos_t - data_real * sin_t)


def forward_transform(signal):
    count = lax.axis_size("seq")
    place = lax.axis_index("seq")
    length, width = signal.shape
    total = 2 * count * length
    pieces = lax.all_to_all(
        signal.reshape(count, length // count, width).astype(jnp.bfloat16),
        "seq",
        split_axis=0,
        concat_axis=0,
        tiled=True,
    ).astype(jnp.float32)
    cos_t, sin_t = angle_table(
        jnp.arange(2 * count, dtype=jnp.int32), jnp.arange(count, dtype=jnp.int32), 2 * count
    )
    mixed_real = jnp.einsum("ka,arc->krc", cos_t, pieces, precision=HIGHEST)
    mixed_imag = jnp.einsum("ka,arc->krc", sin_t, pieces, precision=HIGHEST)
    mixed_real, mixed_imag = (
        lax.all_to_all(
            for_sending(mixed_real), "seq", split_axis=0, concat_axis=1, tiled=True
        ).astype(mixed_real.dtype),
        lax.all_to_all(
            for_sending(mixed_imag), "seq", split_axis=0, concat_axis=1, tiled=True
        ).astype(mixed_imag.dtype),
    )
    freq_index = 2 * place + jnp.arange(2, dtype=jnp.int32)
    return (local_forward(mixed_real, mixed_imag, freq_index, total), freq_index)


def inverse_transform(spectrum, freq_index):
    count = lax.axis_size("seq")
    pair, outer, inner, width = spectrum[0].shape
    length = outer * inner
    total = 2 * count * length
    data_real, data_imag = local_inverse(spectrum[0], spectrum[1], freq_index, total)
    part_real, part_imag = (
        lax.all_to_all(
            for_sending(data_real), "seq", split_axis=1, concat_axis=0, tiled=True
        ).astype(data_real.dtype),
        lax.all_to_all(
            for_sending(data_imag), "seq", split_axis=1, concat_axis=0, tiled=True
        ).astype(data_imag.dtype),
    )
    cos_t, sin_t = angle_table(
        jnp.arange(2 * count, dtype=jnp.int32), jnp.arange(count, dtype=jnp.int32), 2 * count
    )
    signal = (
        jnp.einsum("ka,krc->arc", cos_t, part_real, precision=HIGHEST)
        + jnp.einsum("ka,krc->arc", sin_t, part_imag, precision=HIGHEST)
    ) / (2 * count)
    signal = lax.all_to_all(
        for_sending(signal), "seq", split_axis=0, concat_axis=0, tiled=True
    ).astype(signal.dtype)
    return signal.reshape(length, width)


def split_spec(spectrum, width):
    first = (spectrum[0][..., :width], spectrum[1][..., :width])
    second = (spectrum[0][..., width:], spectrum[1][..., width:])
    return (first, second)


def times_spec(left, right):
    return (left[0] * right[0] - left[1] * right[1], left[0] * right[1] + left[1] * right[0])


def conj_times(left, right):
    return (left[0] * right[0] + left[1] * right[1], left[0] * right[1] - left[1] * right[0])


def per_device(queries, values, filt, w_out, cotangent):
    query = queries[0].astype(jnp.float32)
    value = values[0].astype(jnp.float32)
    width = filt.shape[1]
    joined = jnp.concatenate([value, filt], axis=1)
    spectrum, freq_index = forward_transform(joined)
    value_spec, filt_spec = split_spec(spectrum, width)
    conv = inverse_transform(times_spec(value_spec, filt_spec), freq_index)
    gated = (query * conv).astype(jnp.bfloat16)
    partial_sum = jnp.dot(gated, w_out, preferred_element_type=jnp.float32)
    mixed = lax.psum_scatter(
        partial_sum.astype(jnp.bfloat16), "tensor", scatter_dimension=1, tiled=True
    )
    grad_gated = lax.dot_general(
        lax.all_gather(cotangent[0], "tensor", axis=1, tiled=True),
        w_out,
        (((1,), (1,)), ((), ())),
        preferred_element_type=jnp.float32,
    )
    grad_query = (grad_gated * conv).astype(jnp.bfloat16)
    grad_conv = grad_gated * query
    grad_spec = forward_transform(grad_conv)[0]
    back_value = conj_times(filt_spec, grad_spec)
    back_filt = conj_times(value_spec, grad_spec)
    both_spec = (
        jnp.concatenate([back_value[0], back_filt[0]], axis=3),
        jnp.concatenate([back_value[1], back_filt[1]], axis=3),
    )
    result = inverse_transform(both_spec, freq_index)
    grad_value = result[:, :width].astype(jnp.bfloat16)
    grad_filt = lax.psum(result[:, width:].astype(jnp.bfloat16), "dp").astype(jnp.float32)
    return (mixed[None], grad_query[None], grad_value[None], grad_filt)


def solution(mesh):
    placed = (
        P("dp", "seq", "tensor"),
        P("dp", "seq", "tensor"),
        P("seq", "tensor"),
        P("tensor", None),
        P("dp", "seq", "tensor"),
    )
    return jax.shard_map(
        per_device,
        mesh=mesh,
        in_specs=placed,
        out_specs=(
            P("dp", "seq", "tensor"),
            P("dp", "seq", "tensor"),
            P("dp", "seq", "tensor"),
            P("seq", "tensor"),
        ),
        check_vma=False,
    )
```

profile of v0, /device:TPU:1, one launch (start us, length us, event | category | flops | bytes accessed | tf_op | source)
XLA Modules:
  0.0 429.1 jit_solution(16543263097162809174)
XLA Ops:
  9.8 30.7 %all_to_all.128 = bf16[32,16,256]{2,1,0:T(8,128)(2,1)S(1)} all-to-all(bf16[32,16,256]{2,1,0:T(8,128)(2,1)S(1)} %bitcast.303), channel_id=1, replica_groups=mesh['dp'=4,'seq'=32,'tensor'=4] {'seq'}, dimensions={0} | all-to-all | bytes 524288 | tf_op jit(solution)/shard_map/all_to_all | solution.py:105
  42.3 5.8 %all-to-all-start.1 = ((bf16[64,16,256]{2,1,0:T(8,128)(2,1)}), bf16[64,16,256]{2,1,0:T(8,128)(2,1)S(1)}, u32[]{:S(2)}, u32[]{:S(2)}) async-start(bf16[64,16,256]{2,1,0:T(8,128)(2,1)} %copy.71), calls=%async_computation.1 | async-start | bytes 1048576 | tf_op jit(solution)/shard_map/all_to_all | solution.py:118
  49.9 14.1 %all-to-all-done.1 = bf16[64,16,256]{2,1,0:T(8,128)(2,1)S(1)} async-done(((bf16[64,16,256]{2,1,0:T(8,128)(2,1)}), bf16[64,16,256]{2,1,0:T(8,128)(2,1)S(1)}, u32[]{:S(2)}, u32[]{:S(2)}) %all-to-all-start.1) | async-done | bytes 524320 | tf_op jit(solution)/shard_map/all_to_all | solution.py:118
  64.0 9.6 %all-to-all-start.2 = ((bf16[64,16,256]{2,1,0:T(8,128)(2,1)}), bf16[64,16,256]{2,1,0:T(8,128)(2,1)}, u32[]{:S(2)}, u32[]{:S(2)}) async-start(bf16[64,16,256]{2,1,0:T(8,128)(2,1)} %copy.74), calls=%async_computation.2 | async-start | bytes 1048576 | tf_op jit(solution)/shard_map/all_to_all | solution.py:121
  74.3 15.0 %all-to-all-done.2 = bf16[64,16,256]{2,1,0:T(8,128)(2,1)} async-done(((bf16[64,16,256]{2,1,0:T(8,128)(2,1)}), bf16[64,16,256]{2,1,0:T(8,128)(2,1)}, u32[]{:S(2)}, u32[]{:S(2)}) %all-to-all-start.2) | async-done | bytes 524320 | tf_op jit(solution)/shard_map/all_to_all | solution.py:121
  90.5 2.4 fusion.61
  95.2 2.4 fusion.7
  97.7 3.8 multiply_subtract_fusion
  101.5 4.3 fusion.58
  105.8 9.8 %all-to-all-start.6 = ((bf16[32,16,128]{2,1,0:T(8,128)(2,1)}), bf16[32,16,128]{2,1,0:T(8,128)(2,1)S(1)}, u32[]{:S(2)}, u32[]{:S(2)}) async-start(bf16[32,16,128]{2,1,0:T(8,128)(2,1)} %bitcast.55), calls=%async_computation.7 | async-start | bytes 262144 | tf_op jit(solution)/shard_map/all_to_all | solution.py:105
  115.6 2.6 fusion.34
  118.2 9.6 %all-to-all-done.6 = bf16[32,16,128]{2,1,0:T(8,128)(2,1)S(1)} async-done(((bf16[32,16,128]{2,1,0:T(8,128)(2,1)}), bf16[32,16,128]{2,1,0:T(8,128)(2,1)S(1)}, u32[]{:S(2)}, u32[]{:S(2)}) %all-to-all-start.6) | async-done | bytes 131104 | tf_op jit(solution)/shard_map/all_to_all | solution.py:105
  129.2 4.6 %all-to-all-start.7 = ((bf16[64,16,128]{2,1,0:T(8,128)(2,1)}), bf16[64,16,128]{2,1,0:T(8,128)(2,1)}, u32[]{:S(2)}, u32[]{:S(2)}) async-start(bf16[64,16,128]{2,1,0:T(8,128)(2,1)} %copy.96), calls=%async_computation.8 | async-start | bytes 524288 | tf_op jit(solution)/shard_map/all_to_all | solution.py:118
  133.9 3.8 fusion.5
  139.1 8.6 %all-to-all-done.7 = bf16[64,16,128]{2,1,0:T(8,128)(2,1)} async-done(((bf16[64,16,128]{2,1,0:T(8,128)(2,1)}), bf16[64,16,128]{2,1,0:T(8,128)(2,1)}, u32[]{:S(2)}, u32[]{:S(2)}) %all-to-all-start.7) | async-done | bytes 262176 | tf_op jit(solution)/shard_map/all_to_all | solution.py:118
  147.7 5.8 %all-to-all-start.8 = ((bf16[64,16,128]{2,1,0:T(8,128)(2,1)}), bf16[64,16,128]{2,1,0:T(8,128)(2,1)S(1)}, u32[]{:S(2)}, u32[]{:S(2)}) async-start(bf16[64,16,128]{2,1,0:T(8,128)(2,1)} %copy.99), calls=%async_computation.9 | async-start | bytes 524288 | tf_op jit(solution)/shard_map/all_to_all | solution.py:121
  157.8 9.4 %all-to-all-done.8 = bf16[64,16,128]{2,1,0:T(8,128)(2,1)S(1)} async-done(((bf16[64,16,128]{2,1,0:T(8,128)(2,1)}), bf16[64,16,128]{2,1,0:T(8,128)(2,1)S(1)}, u32[]{:S(2)}, u32[]{:S(2)}) %all-to-all-start.8) | async-done | bytes 262176 | tf_op jit(solution)/shard_map/all_to_all | solution.py:121
  192.9 5.8 %all-to-all-start.10 = ((bf16[2,512,256]{2,0,1:T(2,128)(2,1)}), bf16[2,512,256]{2,0,1:T(2,128)(2,1)S(1)}, u32[]{:S(2)}, u32[]{:S(2)}) async-start(bf16[2,512,256]{2,0,1:T(2,128)(2,1)} %copy.116), calls=%async_computation.11 | async-start | bytes 1048576 | tf_op jit(solution)/shard_map/all_to_all | solution.py:139
  203.8 10.6 %all-to-all-done.10 = bf16[2,512,256]{2,0,1:T(2,128)(2,1)S(1)} async-done(((bf16[2,512,256]{2,0,1:T(2,128)(2,1)}), bf16[2,512,256]{2,0,1:T(2,128)(2,1)S(1)}, u32[]{:S(2)}, u32[]{:S(2)}) %all-to-all-start.10) | async-done | bytes 524320 | tf_op jit(solution)/shard_map/all_to_all | solution.py:139
  214.5 9.3 %all-to-all-start.9 = ((bf16[2,512,256]{2,0,1:T(2,128)(2,1)}), bf16[2,512,256]{2,0,1:T(2,128)(2,1)}, u32[]{:S(2)}, u32[]{:S(2)}) async-start(bf16[2,512,256]{2,0,1:T(2,128)(2,1)} %copy.113), calls=%async_computation.10 | async-start | bytes 1048576 | tf_op jit(solution)/shard_map/all_to_all | solution.py:136
  228.1 11.6 %all-to-all-done.9 = bf16[2,512,256]{2,0,1:T(2,128)(2,1)} async-done(((bf16[2,512,256]{2,0,1:T(2,128)(2,1)}), bf16[2,512,256]{2,0,1:T(2,128)(2,1)}, u32[]{:S(2)}, u32[]{:S(2)}) %all-to-all-start.9) | async-done | bytes 524320 | tf_op jit(solution)/shard_map/all_to_all | solution.py:136
  239.7 9.6 %all-to-all-start.4 = ((bf16[2,512,128]{2,0,1:T(2,128)(2,1)}), bf16[2,512,128]{2,0,1:T(2,128)(2,1)S(1)}, u32[]{:S(2)}, u32[]{:S(2)}) async-start(bf16[2,512,128]{2,0,1:T(2,128)(2,1)} %copy.91), calls=%async_computation.4 | async-start | bytes 524288 | tf_op jit(solution)/shard_map/all_to_all | solution.py:139
  253.0 9.8 %all-to-all-done.4 = bf16[2,512,128]{2,0,1:T(2,128)(2,1)S(1)} async-done(((bf16[2,512,128]{2,0,1:T(2,128)(2,1)}), bf16[2,512,128]{2,0,1:T(2,128)(2,1)S(1)}, u32[]{:S(2)}, u32[]{:S(2)}) %all-to-all-start.4) | async-done | bytes 262176 | tf_op jit(solution)/shard_map/all_to_all | solution.py:139
  262.8 5.8 %all-to-all-start.3 = ((bf16[2,512,128]{2,0,1:T(2,128)(2,1)}), bf16[2,512,128]{2,0,1:T(2,128)(2,1)S(1)}, u32[]{:S(2)}, u32[]{:S(2)}) async-start(bf16[2,512,128]{2,0,1:T(2,128)(2,1)} %copy.88), calls=%async_computation.3 | async-start | bytes 524288 | tf_op jit(solution)/shard_map/all_to_all | solution.py:136
  270.4 11.9 %all-to-all-done.3 = bf16[2,512,128]{2,0,1:T(2,128)(2,1)S(1)} async-done(((bf16[2,512,128]{2,0,1:T(2,128)(2,1)}), bf16[2,512,128]{2,0,1:T(2,128)(2,1)S(1)}, u32[]{:S(2)}, u32[]{:S(2)}) %all-to-all-start.3) | async-done | bytes 262176 | tf_op jit(solution)/shard_map/all_to_all | solution.py:136
  282.3 5.8 %all-to-all-start.11 = ((bf16[32,16,256]{2,1,0:T(8,128)(2,1)}), bf16[32,16,256]{2,1,0:T(8,128)(2,1)S(1)}, u32[]{:S(2)}, u32[]{:S(2)}) async-start(bf16[32,16,256]{2,1,0:T(8,128)(2,1)} %copy.119), calls=%async_computation.12 | async-start | bytes 524288 | tf_op jit(solution)/shard_map/all_to_all | solution.py:150
  290.2 11.6 %all-to-all-done.11 = bf16[32,16,256]{2,1,0:T(8,128)(2,1)S(1)} async-done(((bf16[32,16,256]{2,1,0:T(8,128)(2,1)}), bf16[32,16,256]{2,1,0:T(8,128)(2,1)S(1)}, u32[]{:S(2)}, u32[]{:S(2)}) %all-to-all-start.11) | async-done | bytes 262176 | tf_op jit(solution)/shard_map/all_to_all | solution.py:150
  301.8 5.8 %all-to-all-start.5 = ((bf16[32,16,128]{2,1,0:T(8,128)(2,1)}), bf16[32,16,128]{2,1,0:T(8,128)(2,1)S(1)}, u32[]{:S(2)}, u32[]{:S(2)}) async-start(bf16[32,16,128]{2,1,0:T(8,128)(2,1)} %copy.94), calls=%async_computation.5 | async-start | bytes 262144 | tf_op jit(solution)/shard_map/all_to_all | solution.py:150
  308.4 11.5 %all-to-all-done.5 = bf16[32,16,128]{2,1,0:T(8,128)(2,1)S(1)} async-done(((bf16[32,16,128]{2,1,0:T(8,128)(2,1)}), bf16[32,16,128]{2,1,0:T(8,128)(2,1)S(1)}, u32[]{:S(2)}, u32[]{:S(2)}) %all-to-all-start.5) | async-done | bytes 131104 | tf_op jit(solution)/shard_map/all_to_all | solution.py:150
  320.0 3.2 convolution_convert_fusion
  323.9 41.7 %all-reduce.2.cloned.1.call-done = bf16[512,128]{1,0:T(8,128)(2,1)} async-done(((bf16[512,128]{1,0:T(8,128)(2,1)}), bf16[512,128]{1,0:T(8,128)(2,1)}) %all-reduce.2.cloned.1.call-update) | async-done | bytes 131088 | tf_op jit(solution)/shard_map/psum | solution.py:200
  367.3 55.0 %reduce-scatter.2.cloned.1.call-done = bf16[512,1024]{1,0:T(8,128)(2,1)} async-done(((bf16[512,4096]{1,0:T(8,128)(2,1)}), bf16[512,1024]{1,0:T(8,128)(2,1)}) %reduce-scatter.2.cloned.1.call-update) | async-done | bytes 1048592 | tf_op jit(solution)/shard_map/reduce_scatter | solution.py:180
  (96 shorter events, 62.9 us)
Async XLA Ops:
  7.2 94.4 %copy-start = (bf16[128,4096]{1,0:T(8,128)(2,1)S(1)}, bf16[128,4096]{1,0:T(8,128)(2,1)}, u32[]{:S(2)}) copy-start(bf16[128,4096]{1,0:T(8,128)(2,1)} %param.8) | copy-start | bytes 3145732
  7.2 94.3 %all-gather.3.cloned.1.call-start = ((), (), s32[]{:S(2)}) async-start(), calls=%async_computation.15 | async-start | bytes 5242880 | tf_op jit(solution)/shard_map/all_gather | solution.py:184
  42.3 21.7 %all-to-all-start.1 = ((bf16[64,16,256]{2,1,0:T(8,128)(2,1)}), bf16[64,16,256]{2,1,0:T(8,128)(2,1)S(1)}, u32[]{:S(2)}, u32[]{:S(2)}) async-start(bf16[64,16,256]{2,1,0:T(8,128)(2,1)} %copy.71), calls=%async_computation.1 | async-start | bytes 1048576 | tf_op jit(solution)/shard_map/all_to_all | solution.py:118
  64.0 25.3 %all-to-all-start.2 = ((bf16[64,16,256]{2,1,0:T(8,128)(2,1)}), bf16[64,16,256]{2,1,0:T(8,128)(2,1)}, u32[]{:S(2)}, u32[]{:S(2)}) async-start(bf16[64,16,256]{2,1,0:T(8,128)(2,1)} %copy.74), calls=%async_computation.2 | async-start | bytes 1048576 | tf_op jit(solution)/shard_map/all_to_all | solution.py:121
  97.7 3.9 copy-start.4
  101.5 32.4 %copy-start.1 = (f32[2,32,16,256]{3,1,2,0:T(8,128)S(1)}, f32[2,32,16,256]{3,1,2,0:T(8,128)}, u32[]{:S(2)}) copy-start(f32[2,32,16,256]{3,1,2,0:T(8,128)} %get-tuple-element.11) | copy-start | bytes 3145732
  105.8 22.0 %all-to-all-start.6 = ((bf16[32,16,128]{2,1,0:T(8,128)(2,1)}), bf16[32,16,128]{2,1,0:T(8,128)(2,1)S(1)}, u32[]{:S(2)}, u32[]{:S(2)}) async-start(bf16[32,16,128]{2,1,0:T(8,128)(2,1)} %bitcast.55), calls=%async_computation.7 | async-start | bytes 262144 | tf_op jit(solution)/shard_map/all_to_all | solution.py:105
  129.2 18.4 %all-to-all-start.7 = ((bf16[64,16,128]{2,1,0:T(8,128)(2,1)}), bf16[64,16,128]{2,1,0:T(8,128)(2,1)}, u32[]{:S(2)}, u32[]{:S(2)}) async-start(bf16[64,16,128]{2,1,0:T(8,128)(2,1)} %copy.96), calls=%async_computation.8 | async-start | bytes 524288 | tf_op jit(solution)/shard_map/all_to_all | solution.py:118
  147.7 19.5 %all-to-all-start.8 = ((bf16[64,16,128]{2,1,0:T(8,128)(2,1)}), bf16[64,16,128]{2,1,0:T(8,128)(2,1)S(1)}, u32[]{:S(2)}, u32[]{:S(2)}) async-start(bf16[64,16,128]{2,1,0:T(8,128)(2,1)} %copy.99), calls=%async_computation.9 | async-start | bytes 524288 | tf_op jit(solution)/shard_map/all_to_all | solution.py:121
  169.8 5.5 %copy-start.2 = (f32[2,32,16,256]{3,2,1,0:T(8,128)S(1)}, f32[2,32,16,256]{3,2,1,0:T(8,128)}, u32[]{:S(2)}) copy-start(f32[2,32,16,256]{3,2,1,0:T(8,128)} %fusion.5) | copy-start | bytes 3145732
  192.9 21.6 %all-to-all-start.10 = ((bf16[2,512,256]{2,0,1:T(2,128)(2,1)}), bf16[2,512,256]{2,0,1:T(2,128)(2,1)S(1)}, u32[]{:S(2)}, u32[]{:S(2)}) async-start(bf16[2,512,256]{2,0,1:T(2,128)(2,1)} %copy.116), calls=%async_computation.11 | async-start | bytes 1048576 | tf_op jit(solution)/shard_map/all_to_all | solution.py:139
  214.5 25.2 %all-to-all-start.9 = ((bf16[2,512,256]{2,0,1:T(2,128)(2,1)}), bf16[2,512,256]{2,0,1:T(2,128)(2,1)}, u32[]{:S(2)}, u32[]{:S(2)}) async-start(bf16[2,512,256]{2,0,1:T(2,128)(2,1)} %copy.113), calls=%async_computation.10 | async-start | bytes 1048576 | tf_op jit(solution)/shard_map/all_to_all | solution.py:136
  239.7 23.1 %all-to-all-start.4 = ((bf16[2,512,128]{2,0,1:T(2,128)(2,1)}), bf16[2,512,128]{2,0,1:T(2,128)(2,1)S(1)}, u32[]{:S(2)}, u32[]{:S(2)}) async-start(bf16[2,512,128]{2,0,1:T(2,128)(2,1)} %copy.91), calls=%async_computation.4 | async-start | bytes 524288 | tf_op jit(solution)/shard_map/all_to_all | solution.py:139
  253.0 67.0 %copy-start.5 = (bf16[1,512,128]{2,1,0:T(8,128)(2,1)S(1)}, bf16[1,512,128]{2,1,0:T(8,128)(2,1)}, u32[]{:S(2)}) copy-start(bf16[1,512,128]{2,1,0:T(8,128)(2,1)} %param.5) | copy-start | bytes 393220
  262.8 19.5 %all-to-all-start.3 = ((bf16[2,512,128]{2,0,1:T(2,128)(2,1)}), bf16[2,512,128]{2,0,1:T(2,128)(2,1)S(1)}, u32[]{:S(2)}, u32[]{:S(2)}) async-start(bf16[2,512,128]{2,0,1:T(2,128)(2,1)} %copy.88), calls=%async_computation.3 | async-start | bytes 524288 | tf_op jit(solution)/shard_map/all_to_all | solution.py:136
  282.3 19.5 %all-to-all-start.11 = ((bf16[32,16,256]{2,1,0:T(8,128)(2,1)}), bf16[32,16,256]{2,1,0:T(8,128)(2,1)S(1)}, u32[]{:S(2)}, u32[]{:S(2)}) async-start(bf16[32,16,256]{2,1,0:T(8,128)(2,1)} %copy.119), calls=%async_computation.12 | async-start | bytes 524288 | tf_op jit(solution)/shard_map/all_to_all | solution.py:150
  301.8 18.2 %all-to-all-start.5 = ((bf16[32,16,128]{2,1,0:T(8,128)(2,1)}), bf16[32,16,128]{2,1,0:T(8,128)(2,1)S(1)}, u32[]{:S(2)}, u32[]{:S(2)}) async-start(bf16[32,16,128]{2,1,0:T(8,128)(2,1)} %copy.94), calls=%async_computation.5 | async-start | bytes 262144 | tf_op jit(solution)/shard_map/all_to_all | solution.py:150
  307.6 58.1 %all-reduce.2.cloned.1.call-start = ((), (), s32[]{:S(2)}) async-start(), calls=%async_computation.14 | async-start | bytes 262144 | tf_op jit(solution)/shard_map/psum | solution.py:200
  308.4 113.9 %reduce-scatter.2.cloned.1.call-start = ((), (), s32[]{:S(2)}) async-start(), calls=%async_computation.13 | async-start | bytes 5242880 | tf_op jit(solution)/shard_map/reduce_scatter | solution.py:180
  320.0 3.3 copy-start.3
Sparse Core Ops, SparseCore 0:
  10.1 59.0 all-gather.2
  311.4 54.2 all-reduce.1
  369.3 52.8 reduce-scatter.1
where the time goes:
time: 433 us; the launch traced here: 429 us
  waiting for transfers between devices  221 us (51%)
  starting transfers between devices  78.1 us (18%)
  matrix products  59 us (14%)
  blocking collectives  30.7 us (7%)
  local copies, waits for them, and re-layouts  17.2 us (4%)
  between operations  14.6 us (3%)
  other arithmetic  8.43 us (2%)
    reduce_scatter x1, waiting for transfers between devices, per_device(): lax.psum_scatter(partial_sum.astype(jnp.bfloat16), 'tensor', scatter_dime...  55 us
    dot_general x32, matrix products, apply(): return jnp.einsum(form, left, right, precision=HIGHEST)  47.5 us
    psum x1, waiting for transfers between devices, per_device(): lax.psum(result[:, width:].astype(jnp.bfloat16), 'dp').astype(jnp.float32)  41.7 us
    all_to_all x1, blocking collectives, forward_transform(): lax.all_to_all(signal.reshape(count, length // count, width).astype(jnp.b...  30.7 us
    all_to_all x2, waiting for transfers between devices, forward_transform(): lax.all_to_all(for_sending(mixed_imag), 'seq', split_axis=0, concat_axis=...  24.4 us
    all_to_all x2, waiting for transfers between devices, inverse_transform(): lax.all_to_all(for_sending(data_real), 'seq', split_axis=1, concat_axis=0...  23.5 us
    all_to_all x2, waiting for transfers between devices, inverse_transform(): lax.all_to_all(for_sending(signal), 'seq', split_axis=0, concat_axis=0, t...  23.1 us
    all_to_all x2, waiting for transfers between devices, forward_transform(): lax.all_to_all(for_sending(mixed_real), 'seq', split_axis=0, concat_axis=...  22.7 us
  transfers between devices with their start and end apart: 14, of which 13 were waited for; matrix products, arithmetic and copies ran while one was open for 12% of the time, Pallas kernels for 0%

commit v1 on v0

--- a/solution.py
+++ b/solution.py
@@ -5,6 +5,12 @@
 from jax.sharding import PartitionSpec as P
 
 HIGHEST = lax.Precision.HIGHEST
+
+
+def summed_here(array, mesh_axis):
+    shards = lax.all_gather(array, mesh_axis, axis=0, tiled=False)
+    total = shards.sum(axis=0)
+    return total
 
 
 def for_sending(array):
@@ -197,7 +203,7 @@
     )
     result = inverse_transform(both_spec, freq_index)
     grad_value = result[:, :width].astype(jnp.bfloat16)
-    grad_filt = lax.psum(result[:, width:].astype(jnp.bfloat16), "dp").astype(jnp.float32)
+    grad_filt = summed_here(result[:, width:].astype(jnp.bfloat16), "dp").astype(jnp.float32)
     return (mixed[None], grad_query[None], grad_value[None], grad_filt)
 
 

time: 433 us -> 364 us (0.84)
  the two profiles are of different devices: /device:TPU:1 before, /device:TPU:2 now
where the time goes in v1:
time: 364 us; the launch traced here: 360 us
  waiting for transfers between devices  133 us (37%)
  blocking collectives  67 us (18%)
  starting transfers between devices  60.1 us (17%)
  matrix products  60 us (16%)
  local copies, waits for them, and re-layouts  16.4 us (5%)
  between operations  15 us (4%)
  other arithmetic  8.11 us (2%)
    dot_general x32, matrix products, apply(): return jnp.einsum(form, left, right, precision=HIGHEST)  48.6 us
    all_to_all x2, waiting for transfers between devices, inverse_transform(): lax.all_to_all(for_sending(data_real), 'seq', split_axis=1, concat_axis=0...  30.6 us
    all_to_all x1, blocking collectives, forward_transform(): lax.all_to_all(signal.reshape(count, length // count, width).astype(jnp.b...  29.8 us
    all_to_all x2, waiting for transfers between devices, inverse_transform(): lax.all_to_all(for_sending(data_imag), 'seq', split_axis=1, concat_axis=0...  28.6 us
    all_to_all x2, waiting for transfers between devices, forward_transform(): lax.all_to_all(for_sending(mixed_imag), 'seq', split_axis=0, concat_axis=...  25.4 us
    all_to_all x2, waiting for transfers between devices, forward_transform(): lax.all_to_all(for_sending(mixed_real), 'seq', split_axis=0, concat_axis=...  24.7 us
    all_gather x1, blocking collectives, summed_here(): shards = lax.all_gather(array, mesh_axis, axis=0, tiled=False)  19.2 us
    all_to_all x1, blocking collectives, inverse_transform(): lax.all_to_all(for_sending(signal), 'seq', split_axis=0, concat_axis=0, t...  18 us
  transfers between devices with their start and end apart: 12, of which 10 were waited for; matrix products, arithmetic and copies ran while one was open for 15% of the time, Pallas kernels for 0%

profile of v1, /device:TPU:2, one launch (start us, length us, event | category | flops | bytes accessed | tf_op | source)
XLA Modules:
  0.0 359.8 jit_solution(6267958248809366986)
XLA Ops:
  9.8 29.8 %all_to_all.128 = bf16[32,16,256]{2,1,0:T(8,128)(2,1)S(1)} all-to-all(bf16[32,16,256]{2,1,0:T(8,128)(2,1)S(1)} %bitcast.305), channel_id=1, replica_groups=mesh['dp'=4,'seq'=32,'tensor'=4] {'seq'}, dimensions={0} | all-to-all | bytes 524288 | tf_op jit(solution)/shard_map/all_to_all | solution.py:111
  41.4 5.4 %all-to-all-start.1 = ((bf16[64,16,256]{2,1,0:T(8,128)(2,1)}), bf16[64,16,256]{2,1,0:T(8,128)(2,1)S(1)}, u32[]{:S(2)}, u32[]{:S(2)}) async-start(bf16[64,16,256]{2,1,0:T(8,128)(2,1)} %copy.71), calls=%async_computation.1 | async-start | bytes 1048576 | tf_op jit(solution)/shard_map/all_to_all | solution.py:124
  48.7 16.1 %all-to-all-done.1 = bf16[64,16,256]{2,1,0:T(8,128)(2,1)S(1)} async-done(((bf16[64,16,256]{2,1,0:T(8,128)(2,1)}), bf16[64,16,256]{2,1,0:T(8,128)(2,1)S(1)}, u32[]{:S(2)}, u32[]{:S(2)}) %all-to-all-start.1) | async-done | bytes 524320 | tf_op jit(solution)/shard_map/all_to_all | solution.py:124
  64.7 7.5 %all-to-all-start.2 = ((bf16[64,16,256]{2,1,0:T(8,128)(2,1)}), bf16[64,16,256]{2,1,0:T(8,128)(2,1)}, u32[]{:S(2)}, u32[]{:S(2)}) async-start(bf16[64,16,256]{2,1,0:T(8,128)(2,1)} %copy.74), calls=%async_computation.2 | async-start | bytes 1048576 | tf_op jit(solution)/shard_map/all_to_all | solution.py:127
  73.5 16.7 %all-to-all-done.2 = bf16[64,16,256]{2,1,0:T(8,128)(2,1)} async-done(((bf16[64,16,256]{2,1,0:T(8,128)(2,1)}), bf16[64,16,256]{2,1,0:T(8,128)(2,1)}, u32[]{:S(2)}, u32[]{:S(2)}) %all-to-all-start.2) | async-done | bytes 524320 | tf_op jit(solution)/shard_map/all_to_all | solution.py:127
  91.4 2.4 fusion.61
  93.8 2.4 fusion.65
  96.2 2.4 fusion.7
  98.6 3.8 %multiply_subtract_fusion = (f32[2,32,16,256]{3,1,2,0:T(8,128)S(1)}, f32[2,32,16,256]{3,1,2,0:T(8,128)}) fusion(f32[2,32,16,256]{3,1,2,0:T(8,128)S(1)} %fusion.7, f32[32,16]{0,1:T(8,128)S(1)} %get-tuple-element.30, f32[32,16]{0,1:T(8,128)S(1)} %get-tuple-element.31, f32[2,16,256,32]{2,3,1,0:T(8,128)S(1)} %fusion.61, f32[32,2,16,256]{3,2,1,0:T(8,128)S(1)} %convert.23, ...), kind=kOutput, calls=%fused_computation.60 | convolution fusion | flops 103299072 | bytes 6303744 | tf_op jit(solution)/shard_map/ab,ebcd->eacd/dot_general | solution.py:29
  102.5 4.3 %fusion.58 = (bf16[512,128]{1,0:T(8,128)(2,1)}, f32[512,128]{1,0:T(8,128)}) fusion(bf16[1,512,128]{2,1,0:T(8,128)(2,1)S(1)} %copy-done.5, bf16[128,4096]{1,0:T(8,128)(2,1)S(1)} %copy-done, bf16[1,512,4096]{2,1,0:T(8,128)(2,1)} %all-gather.4.cloned.1.call-done), kind=kOutput, calls=%fused_computation.116 | convolution fusion | flops 537067520 | bytes 5767168 | tf_op jit(solution)/shard_map/dot_general | solution.py:189
  106.8 7.4 %all-to-all-start.6 = ((bf16[32,16,128]{2,1,0:T(8,128)(2,1)}), bf16[32,16,128]{2,1,0:T(8,128)(2,1)S(1)}, u32[]{:S(2)}, u32[]{:S(2)}) async-start(bf16[32,16,128]{2,1,0:T(8,128)(2,1)} %bitcast.55), calls=%async_computation.7 | async-start | bytes 262144 | tf_op jit(solution)/shard_map/all_to_all | solution.py:111
  114.2 2.6 fusion.34
  116.8 10.0 %all-to-all-done.6 = bf16[32,16,128]{2,1,0:T(8,128)(2,1)S(1)} async-done(((bf16[32,16,128]{2,1,0:T(8,128)(2,1)}), bf16[32,16,128]{2,1,0:T(8,128)(2,1)S(1)}, u32[]{:S(2)}, u32[]{:S(2)}) %all-to-all-start.6) | async-done | bytes 131104 | tf_op jit(solution)/shard_map/all_to_all | solution.py:111
  128.2 4.6 %all-to-all-start.7 = ((bf16[64,16,128]{2,1,0:T(8,128)(2,1)}), bf16[64,16,128]{2,1,0:T(8,128)(2,1)}, u32[]{:S(2)}, u32[]{:S(2)}) async-start(bf16[64,16,128]{2,1,0:T(8,128)(2,1)} %copy.96), calls=%async_computation.8 | async-start | bytes 524288 | tf_op jit(solution)/shard_map/all_to_all | solution.py:124
  132.8 3.9 %fusion.5 = f32[2,32,16,256]{3,2,1,0:T(8,128)} fusion(f32[2,32,256,16]{2,3,1,0:T(8,128)} %fusion.34, f32[2,32,16,256]{3,1,2,0:T(8,128)S(1)} %copy-done.1), kind=kOutput, calls=%fused_computation.12 | convolution fusion | flops 50597376 | bytes 3145728 | tf_op jit(solution)/shard_map/ab,ecbd->ecad/dot_general | solution.py:29
  138.1 8.6 %all-to-all-done.7 = bf16[64,16,128]{2,1,0:T(8,128)(2,1)} async-done(((bf16[64,16,128]{2,1,0:T(8,128)(2,1)}), bf16[64,16,128]{2,1,0:T(8,128)(2,1)}, u32[]{:S(2)}, u32[]{:S(2)}) %all-to-all-start.7) | async-done | bytes 262176 | tf_op jit(solution)/shard_map/all_to_all | solution.py:124
  146.7 5.6 %all-to-all-start.8 = ((bf16[64,16,128]{2,1,0:T(8,128)(2,1)}), bf16[64,16,128]{2,1,0:T(8,128)(2,1)S(1)}, u32[]{:S(2)}, u32[]{:S(2)}) async-start(bf16[64,16,128]{2,1,0:T(8,128)(2,1)} %copy.99), calls=%async_computation.9 | async-start | bytes 524288 | tf_op jit(solution)/shard_map/all_to_all | solution.py:127
  153.9 2.6 fusion.4
  157.5 8.6 %all-to-all-done.8 = bf16[64,16,128]{2,1,0:T(8,128)(2,1)S(1)} async-done(((bf16[64,16,128]{2,1,0:T(8,128)(2,1)}), bf16[64,16,128]{2,1,0:T(8,128)(2,1)S(1)}, u32[]{:S(2)}, u32[]{:S(2)}) %all-to-all-start.8) | async-done | bytes 262176 | tf_op jit(solution)/shard_map/all_to_all | solution.py:127
  184.2 5.6 %all-to-all-start.4 = ((bf16[2,512,128]{2,0,1:T(2,128)(2,1)}), bf16[2,512,128]{2,0,1:T(2,128)(2,1)S(1)}, u32[]{:S(2)}, u32[]{:S(2)}) async-start(bf16[2,512,128]{2,0,1:T(2,128)(2,1)} %copy.91), calls=%async_computation.4 | async-start | bytes 524288 | tf_op jit(solution)/shard_map/all_to_all | solution.py:145
  191.7 11.9 %all-to-all-done.4 = bf16[2,512,128]{2,0,1:T(2,128)(2,1)S(1)} async-done(((bf16[2,512,128]{2,0,1:T(2,128)(2,1)}), bf16[2,512,128]{2,0,1:T(2,128)(2,1)S(1)}, u32[]{:S(2)}, u32[]{:S(2)}) %all-to-all-start.4) | async-done | bytes 262176 | tf_op jit(solution)/shard_map/all_to_all | solution.py:145
  203.7 5.7 %all-to-all-start.3 = ((bf16[2,512,128]{2,0,1:T(2,128)(2,1)}), bf16[2,512,128]{2,0,1:T(2,128)(2,1)}, u32[]{:S(2)}, u32[]{:S(2)}) async-start(bf16[2,512,128]{2,0,1:T(2,128)(2,1)} %copy.88), calls=%async_computation.3 | async-start | bytes 524288 | tf_op jit(solution)/shard_map/all_to_all | solution.py:142
  209.8 13.5 %all-to-all-done.3 = bf16[2,512,128]{2,0,1:T(2,128)(2,1)} async-done(((bf16[2,512,128]{2,0,1:T(2,128)(2,1)}), bf16[2,512,128]{2,0,1:T(2,128)(2,1)}, u32[]{:S(2)}, u32[]{:S(2)}) %all-to-all-start.3) | async-done | bytes 262176 | tf_op jit(solution)/shard_map/all_to_all | solution.py:142
  225.3 18.0 %all_to_all.129 = bf16[32,16,128]{2,1,0:T(8,128)(2,1)S(1)} all-to-all(bf16[32,16,128]{2,1,0:T(8,128)(2,1)S(1)} %copy.94), channel_id=1, replica_groups=mesh['dp'=4,'seq'=32,'tensor'=4] {'seq'}, dimensions={0} | all-to-all | bytes 262144 | tf_op jit(solution)/shard_map/all_to_all | solution.py:156
  243.3 3.2 convolution_convert_fusion
  261.3 4.1 %all-to-all-start.10 = ((bf16[2,512,256]{2,0,1:T(2,128)(2,1)}), bf16[2,512,256]{2,0,1:T(2,128)(2,1)S(1)}, u32[]{:S(2)}, u32[]{:S(2)}) async-start(bf16[2,512,256]{2,0,1:T(2,128)(2,1)} %copy.116), calls=%async_computation.11 | async-start | bytes 1048576 | tf_op jit(solution)/shard_map/all_to_all | solution.py:145
  266.7 16.7 %all-to-all-done.10 = bf16[2,512,256]{2,0,1:T(2,128)(2,1)S(1)} async-done(((bf16[2,512,256]{2,0,1:T(2,128)(2,1)}), bf16[2,512,256]{2,0,1:T(2,128)(2,1)S(1)}, u32[]{:S(2)}, u32[]{:S(2)}) %all-to-all-start.10) | async-done | bytes 524320 | tf_op jit(solution)/shard_map/all_to_all | solution.py:145
  283.4 7.0 %all-to-all-start.9 = ((bf16[2,512,256]{2,0,1:T(2,128)(2,1)}), bf16[2,512,256]{2,0,1:T(2,128)(2,1)S(1)}, u32[]{:S(2)}, u32[]{:S(2)}) async-start(bf16[2,512,256]{2,0,1:T(2,128)(2,1)} %copy.113), calls=%async_computation.10 | async-start | bytes 1048576 | tf_op jit(solution)/shard_map/all_to_all | solution.py:142
  291.3 17.2 %all-to-all-done.9 = bf16[2,512,256]{2,0,1:T(2,128)(2,1)S(1)} async-done(((bf16[2,512,256]{2,0,1:T(2,128)(2,1)}), bf16[2,512,256]{2,0,1:T(2,128)(2,1)S(1)}, u32[]{:S(2)}, u32[]{:S(2)}) %all-to-all-start.9) | async-done | bytes 524320 | tf_op jit(solution)/shard_map/all_to_all | solution.py:142
  311.1 7.0 %all-to-all-start.11 = ((bf16[32,16,256]{2,1,0:T(8,128)(2,1)}), bf16[32,16,256]{2,1,0:T(8,128)(2,1)S(1)}, u32[]{:S(2)}, u32[]{:S(2)}) async-start(bf16[32,16,256]{2,1,0:T(8,128)(2,1)} %copy.119), calls=%async_computation.12 | async-start | bytes 524288 | tf_op jit(solution)/shard_map/all_to_all | solution.py:156
  318.8 13.2 %all-to-all-done.11 = bf16[32,16,256]{2,1,0:T(8,128)(2,1)S(1)} async-done(((bf16[32,16,256]{2,1,0:T(8,128)(2,1)}), bf16[32,16,256]{2,1,0:T(8,128)(2,1)S(1)}, u32[]{:S(2)}, u32[]{:S(2)}) %all-to-all-start.11) | async-done | bytes 262176 | tf_op jit(solution)/shard_map/all_to_all | solution.py:156
  332.7 19.2 %all-gather.1 = bf16[2048,128]{1,0:T(8,128)(2,1)S(1)} all-gather(bf16[512,128]{1,0:T(8,128)(2,1)S(1)} %get-tuple-element.22), channel_id=3, replica_groups=mesh['dp'=4,'seq'=32,'tensor'=4] {'dp'}, dimensions={0}, use_global_device_ids=true | all-gather | bytes 655360 | tf_op jit(solution)/shard_map/all_gather | solution.py:11
  (108 shorter events, 57.7 us)
Async XLA Ops:
  7.2 95.3 %copy-start = (bf16[128,4096]{1,0:T(8,128)(2,1)S(1)}, bf16[128,4096]{1,0:T(8,128)(2,1)}, u32[]{:S(2)}) copy-start(bf16[128,4096]{1,0:T(8,128)(2,1)} %param.8) | copy-start | bytes 3145732
  7.2 95.3 %all-gather.4.cloned.1.call-start = ((), (), s32[]{:S(2)}) async-start(), calls=%async_computation.14 | async-start | bytes 5242880 | tf_op jit(solution)/shard_map/all_gather | solution.py:190
  41.4 23.3 %all-to-all-start.1 = ((bf16[64,16,256]{2,1,0:T(8,128)(2,1)}), bf16[64,16,256]{2,1,0:T(8,128)(2,1)S(1)}, u32[]{:S(2)}, u32[]{:S(2)}) async-start(bf16[64,16,256]{2,1,0:T(8,128)(2,1)} %copy.71), calls=%async_computation.1 | async-start | bytes 1048576 | tf_op jit(solution)/shard_map/all_to_all | solution.py:124
  64.7 25.5 %all-to-all-start.2 = ((bf16[64,16,256]{2,1,0:T(8,128)(2,1)}), bf16[64,16,256]{2,1,0:T(8,128)(2,1)}, u32[]{:S(2)}, u32[]{:S(2)}) async-start(bf16[64,16,256]{2,1,0:T(8,128)(2,1)} %copy.74), calls=%async_computation.2 | async-start | bytes 1048576 | tf_op jit(solution)/shard_map/all_to_all | solution.py:127
  72.5 105.1 %copy-start.7 = (f32[32,16]{1,0:T(8,128)}, f32[32,16]{1,0:T(8,128)S(1)}, u32[]{:S(2)}) copy-start(f32[32,16]{1,0:T(8,128)S(1)} %copy.80) | copy-start | bytes 6148
  98.6 3.9 %copy-start.5 = (bf16[1,512,128]{2,1,0:T(8,128)(2,1)S(1)}, bf16[1,512,128]{2,1,0:T(8,128)(2,1)}, u32[]{:S(2)}) copy-start(bf16[1,512,128]{2,1,0:T(8,128)(2,1)} %param.5) | copy-start | bytes 393220
  102.5 30.3 %copy-start.1 = (f32[2,32,16,256]{3,1,2,0:T(8,128)S(1)}, f32[2,32,16,256]{3,1,2,0:T(8,128)}, u32[]{:S(2)}) copy-start(f32[2,32,16,256]{3,1,2,0:T(8,128)} %get-tuple-element.11) | copy-start | bytes 3145732
  106.8 20.0 %all-to-all-start.6 = ((bf16[32,16,128]{2,1,0:T(8,128)(2,1)}), bf16[32,16,128]{2,1,0:T(8,128)(2,1)S(1)}, u32[]{:S(2)}, u32[]{:S(2)}) async-start(bf16[32,16,128]{2,1,0:T(8,128)(2,1)} %bitcast.55), calls=%async_computation.7 | async-start | bytes 262144 | tf_op jit(solution)/shard_map/all_to_all | solution.py:111
  128.2 18.5 %all-to-all-start.7 = ((bf16[64,16,128]{2,1,0:T(8,128)(2,1)}), bf16[64,16,128]{2,1,0:T(8,128)(2,1)}, u32[]{:S(2)}, u32[]{:S(2)}) async-start(bf16[64,16,128]{2,1,0:T(8,128)(2,1)} %copy.96), calls=%async_computation.8 | async-start | bytes 524288 | tf_op jit(solution)/shard_map/all_to_all | solution.py:124
  146.7 19.5 %all-to-all-start.8 = ((bf16[64,16,128]{2,1,0:T(8,128)(2,1)}), bf16[64,16,128]{2,1,0:T(8,128)(2,1)S(1)}, u32[]{:S(2)}, u32[]{:S(2)}) async-start(bf16[64,16,128]{2,1,0:T(8,128)(2,1)} %copy.99), calls=%async_computation.9 | async-start | bytes 524288 | tf_op jit(solution)/shard_map/all_to_all | solution.py:127
  168.8 5.5 %copy-start.2 = (f32[2,32,16,256]{3,2,1,0:T(8,128)S(1)}, f32[2,32,16,256]{3,2,1,0:T(8,128)}, u32[]{:S(2)}) copy-start(f32[2,32,16,256]{3,2,1,0:T(8,128)} %fusion.5) | copy-start | bytes 3145732
  168.8 5.5 %copy-start.3 = (f32[2,32,16,256]{3,2,1,0:T(8,128)S(1)}, f32[2,32,16,256]{3,2,1,0:T(8,128)}, u32[]{:S(2)}) copy-start(f32[2,32,16,256]{3,2,1,0:T(8,128)} %fusion.4) | copy-start | bytes 3145732
  178.4 3.8 %copy-start.9 = (f32[2,512]{1,0:T(2,128)S(1)}, f32[2,512]{1,0:T(2,128)}, u32[]{:S(2)}) copy-start(f32[2,512]{1,0:T(2,128)} %get-tuple-element.26) | copy-start | bytes 12292
  178.4 3.8 %copy-start.11 = (f32[2,512]{1,0:T(2,128)S(1)}, f32[2,512]{1,0:T(2,128)}, u32[]{:S(2)}) copy-start(f32[2,512]{1,0:T(2,128)} %get-tuple-element.27) | copy-start | bytes 12292
  181.8 61.4 %copy-start.6 = (bf16[1,512,128]{2,1,0:T(8,128)(2,1)S(1)}, bf16[1,512,128]{2,1,0:T(8,128)(2,1)}, u32[]{:S(2)}) copy-start(bf16[1,512,128]{2,1,0:T(8,128)(2,1)} %param.5) | copy-start | bytes 393220
  184.2 19.5 %all-to-all-start.4 = ((bf16[2,512,128]{2,0,1:T(2,128)(2,1)}), bf16[2,512,128]{2,0,1:T(2,128)(2,1)S(1)}, u32[]{:S(2)}, u32[]{:S(2)}) async-start(bf16[2,512,128]{2,0,1:T(2,128)(2,1)} %copy.91), calls=%async_computation.4 | async-start | bytes 524288 | tf_op jit(solution)/shard_map/all_to_all | solution.py:145
  203.7 19.6 %all-to-all-start.3 = ((bf16[2,512,128]{2,0,1:T(2,128)(2,1)}), bf16[2,512,128]{2,0,1:T(2,128)(2,1)}, u32[]{:S(2)}, u32[]{:S(2)}) async-start(bf16[2,512,128]{2,0,1:T(2,128)(2,1)} %copy.88), calls=%async_computation.3 | async-start | bytes 524288 | tf_op jit(solution)/shard_map/all_to_all | solution.py:142
  209.4 143.3 %reduce-scatter.2.cloned.1.call-start = ((), (), s32[]{:S(2)}) async-start(), calls=%async_computation.13 | async-start | bytes 5242880 | tf_op jit(solution)/shard_map/reduce_scatter | solution.py:186
  246.5 3.2 copy-start.8
  255.2 4.3 %copy-start.10 = (f32[2,512]{1,0:T(2,128)S(1)}, f32[2,512]{1,0:T(2,128)}, u32[]{:S(2)}) copy-start(f32[2,512]{1,0:T(2,128)} %get-tuple-element.26) | copy-start | bytes 12292
  255.2 4.3 %copy-start.12 = (f32[2,512]{1,0:T(2,128)S(1)}, f32[2,512]{1,0:T(2,128)}, u32[]{:S(2)}) copy-start(f32[2,512]{1,0:T(2,128)} %get-tuple-element.27) | copy-start | bytes 12292
  261.3 22.1 %all-to-all-start.10 = ((bf16[2,512,256]{2,0,1:T(2,128)(2,1)}), bf16[2,512,256]{2,0,1:T(2,128)(2,1)S(1)}, u32[]{:S(2)}, u32[]{:S(2)}) async-start(bf16[2,512,256]{2,0,1:T(2,128)(2,1)} %copy.116), calls=%async_computation.11 | async-start | bytes 1048576 | tf_op jit(solution)/shard_map/all_to_all | solution.py:145
  283.4 25.1 %all-to-all-start.9 = ((bf16[2,512,256]{2,0,1:T(2,128)(2,1)}), bf16[2,512,256]{2,0,1:T(2,128)(2,1)S(1)}, u32[]{:S(2)}, u32[]{:S(2)}) async-start(bf16[2,512,256]{2,0,1:T(2,128)(2,1)} %copy.113), calls=%async_computation.10 | async-start | bytes 1048576 | tf_op jit(solution)/shard_map/all_to_all | solution.py:142
  290.5 27.6 %copy-start.4 = (f32[512,128]{1,0:T(8,128)S(1)}, f32[512,128]{1,0:T(8,128)}, u32[]{:S(2)}) copy-start(f32[512,128]{1,0:T(8,128)} %get-tuple-element.29) | copy-start | bytes 786436
  311.1 20.9 %all-to-all-start.11 = ((bf16[32,16,256]{2,1,0:T(8,128)(2,1)}), bf16[32,16,256]{2,1,0:T(8,128)(2,1)S(1)}, u32[]{:S(2)}, u32[]{:S(2)}) async-start(bf16[32,16,256]{2,1,0:T(8,128)(2,1)} %copy.119), calls=%async_computation.12 | async-start | bytes 524288 | tf_op jit(solution)/shard_map/all_to_all | solution.py:156
Sparse Core Ops, SparseCore 0:
  10.1 57.5 all-gather.3
  246.6 46.3 reduce-scatter.1
